TPU v7x, 256 devices: a whole 4x4x8 slice. The times are simulated.
256 devices in a mesh: grp: 8 (over y, x_lo), brick: 32 (over z, x_hi, core).
Axes of the slice: x: 4 (x_hi: 2, x_lo: 2; x = x_hi * 2 + x_lo), y: 4, z: 8, core: 2. Of those that a mesh axis runs over, the one named last changes fastest.
Arguments:
- coeffs: bfloat16 [8, 16384, 1024], P(None, 'brick'), may hold values from -6 to 6
- tensor: bfloat16 [32, 1024, 1024], P('grp', 'brick'), may hold values from -0.005859375 to 0.005859375
- pairs: int32 [2, 2], replicated, may hold values from 0 to 7
- lateral: int32 [16384], P('brick'), may hold values from 0 to 511
- thermal: float32 [8], replicated, may hold values from 0.5 to 1
Outputs:
- updated: float32 [32, 8, 16384], P(None, None, 'brick')
Inputs may be any that keep to these rules, and one draw needn't show every extreme that they name: `pairs`: row p names the species that receives the collision term and the species it collides with. A cell's lateral partner, as an index within the same block of 512 cells.
All inputs are finite; a program needn't handle non-finite values.
Results may differ from a plain program's by a relative error of at most 0.0003.
Values may be sent and summed in bfloat16 or wider, within the bound.
No kernel may reach another device: no remote copies, remote signals or barrier semaphores. Data moves between devices by JAX's collectives and lax.ppermute only.
A program may use at most 128 MiB of HBM per device.

v0:
```python
import jax
import jax.numpy as jnp
from jax import lax
from jax.sharding import PartitionSpec as P

PLANE = 128
collision_update = 0.5
courant = 0.08
max_speed = 11.0
mixing = 0.2


def sent_to_all(array, axis):
    copies = jnp.broadcast_to(array, (lax.axis_size(axis), *array.shape))
    return lax.all_to_all(copies, axis, split_axis=0, concat_axis=0, tiled=True)


def in_order(parts, dim):
    shape = list(parts.shape[1:])
    shape[dim] *= parts.shape[0]
    return jnp.moveaxis(parts, 0, dim).reshape(shape)


def gather_directly(array, axis, dim):
    parts = sent_to_all(array, axis)
    return in_order(parts, dim)


def with_halo(cells, sides, width):
    for axis, dim in sides:
        count = lax.axis_size(axis)
        head = lax.slice_in_dim(cells, 0, width, axis=dim)
        tail = lax.slice_in_dim(cells, cells.shape[dim] - width, cells.shape[dim], axis=dim)
        cells = jnp.concatenate(
            [
                lax.ppermute(tail, axis, [(i, (i + 1) % count) for i in range(count)]),
                cells,
                lax.ppermute(head, axis, [((i + 1) % count, i) for i in range(count)]),
            ],
            axis=dim,
        )
    return cells


def advance(extended, thermal, partner):
    mode_count = extended.shape[0] - 2
    thermo = thermal[None, :, None, None]
    orders = jnp.arange(mode_count, dtype=jnp.int32).astype(jnp.float32)[:, None, None, None]
    speed = thermo * (
        jnp.sqrt(orders) * extended[:mode_count] + jnp.sqrt(orders + 1.0) * extended[2:]
    )
    middle = extended[1 : mode_count + 1]
    face = 0.5 * (speed[:, :, :-1] + speed[:, :, 1:]) - 0.5 * max_speed * thermo * (
        middle[:, :, 1:] - middle[:, :, :-1]
    )
    center = middle[:, :, 1:-1]
    shape_flat = (mode_count, center.shape[1], center.shape[2] * center.shape[3])
    center = center.reshape(shape_flat)
    divergence = (face[:, :, 1:] - face[:, :, :-1]).reshape(shape_flat)
    beside = jnp.take(center, partner, axis=2)
    return center - courant * divergence + mixing * (beside - center)


def local(coeffs, tensor, pairs, lateral, thermal):
    species, cells, width = coeffs.shape
    local_modes = tensor.shape[0]
    group_count = lax.axis_size("grp")
    modes = local_modes * group_count
    pair_count = pairs.shape[0]
    layers = cells // PLANE
    left_rows = jnp.transpose(coeffs[pairs[:, 0]], (2, 0, 1))
    right_flat = coeffs[pairs[:, 1]].reshape(pair_count * cells, width)
    brick_window = jnp.transpose(coeffs[:, :, :modes], (2, 0, 1))
    padded_state = jnp.pad(brick_window, ((1, 1), (0, 0), (0, 0)))
    indicator_matrix = (
        pairs[:, 0][:, None] == jnp.arange(species, dtype=jnp.int32)[None, :]
    ).astype(jnp.float32)
    piece = lax.all_gather(tensor, "brick", axis=1, tiled=True)
    rows_here = piece.shape[1]
    inner = lax.dot_general(
        piece.reshape(local_modes * rows_here, width),
        right_flat,
        (((1,), (1,)), ((), ())),
        preferred_element_type=jnp.float32,
    )
    inner = inner.reshape(local_modes, rows_here, pair_count, cells)
    factor = left_rows.astype(jnp.float32)
    collide = jnp.sum(inner * factor[None], axis=1)
    pair_all = gather_directly(collide, "grp", 0)
    pair_extended = jnp.pad(pair_all, ((1, 1), (0, 0), (0, 0)))
    span = pair_extended.shape[0]
    collision_extended = jnp.einsum(
        "quw,ut->qtw", pair_extended, indicator_matrix, precision=lax.Precision.HIGHEST
    )
    species_state = padded_state.astype(jnp.float32) + collision_update * collision_extended
    extended = with_halo(species_state.reshape(span, species, layers, PLANE), (("brick", 2),), 1)
    updated = advance(extended, thermal, lateral)
    return updated


def solution(mesh):
    in_specs = (P(None, "brick", None), P("grp", "brick", None), P(), P("brick"), P())
    out_specs = P(None, None, "brick")
    return jax.shard_map(local, mesh=mesh, in_specs=in_specs, out_specs=out_specs, check_vma=False)
```

profile of v0, /device:TPU:2, one launch (start us, length us, event | category | flops | bytes accessed | tf_op | source)
XLA Modules:
  0.0 193.8 jit_solution(13047162379919570659)
XLA Ops:
  6.5 0.7 all-gather.2.cloned.1.call-update
  7.3 1.0 slice_reduce_fusion
  8.3 5.5 %gather_fusion = bf16[2,512,1024]{2,1,0:T(8,128)(2,1)} fusion(bf16[8,512,1024]{2,1,0:T(8,128)(2,1)} %param.5, s32[1024]{0:T(1024)S(1)} %get-tuple-element.11), kind=kCustom, calls=%fused_computation | custom fusion | bytes 4194312 | tf_op jit(solution)/shard_map/gather | solution.py:72
  13.8 4.1 %gather_fusion.1 = bf16[2,512,1024]{2,1,0:T(8,128)(2,1)S(1)} fusion(bf16[8,512,1024]{2,1,0:T(8,128)(2,1)} %param.5, s32[1024]{0:T(1024)S(1)} %get-tuple-element.10), kind=kCustom, calls=%fused_computation.1 | custom fusion | bytes 4194312 | tf_op jit(solution)/shard_map/gather | solution.py:71
  17.8 0.5 copy.14
  18.4 2.5 %convert_bitcast_fusion = f32[1024,2,512]{0,2,1:T(8,128)} fusion(bf16[2,512,1024]{2,1,0:T(8,128)(2,1)S(1)} %gather_fusion.1), kind=kLoop, calls=%fused_computation.5 | loop fusion | flops 1048576 | bytes 6291456 | tf_op jit(solution)/shard_map/convert_element_type | solution.py:87
  20.9 92.7 %all-gather.2.cloned.1.call-done = bf16[4,1024,1024]{2,1,0:T(8,128)(2,1)} async-done(((bf16[4,32,1024]{2,1,0:T(8,128)(2,1)}), bf16[4,1024,1024]{2,1,0:T(8,128)(2,1)}) %all-gather.2.cloned.1.call-update) | async-done | bytes 8388624 | tf_op jit(solution)/shard_map/all_gather | solution.py:78
  113.7 16.0 %convolution_bitcast_fusion = f32[4096,1024]{0,1:T(8,128)} fusion(bf16[1024,1024]{1,0:T(8,128)(2,1)} %bitcast.35, bf16[4096,1024]{1,0:T(8,128)(2,1)} %bitcast.38), kind=kOutput, calls=%fused_computation.4 | convolution fusion | flops 8589934592 | bytes 27262976 | tf_op jit(solution)/shard_map/dot_general | solution.py:80
  129.7 20.4 %reshape.44 = f32[4,1024,2,512]{1,0,3,2:T(4,128)} reshape(f32[4096,1024]{0,1:T(8,128)} %convolution_bitcast_fusion) | data formatting | bytes 33554432 | tf_op jit(solution)/shard_map/reshape | solution.py:86
  150.1 10.5 %multiply_reduce_fusion = f32[4,2,512]{0,2,1:T(8,128)S(1)} fusion(f32[4,1024,2,512]{1,0,3,2:T(4,128)} %reshape.44, f32[1024,2,512]{0,2,1:T(8,128)} %convert_bitcast_fusion), kind=kLoop, calls=%fused_computation.3 | loop fusion | flops 8384512 | bytes 20987904 | tf_op jit(solution)/shard_map/reduce_sum | solution.py:88
  160.7 0.2 copy.11
  160.9 0.7 broadcast_in_dim.21
  161.6 5.7 %all-to-all-start = ((f32[8,4,2,512]{3,2,1,0:T(2,128)}), f32[8,4,2,512]{3,2,1,0:T(2,128)S(1)}, u32[]{:S(2)}, u32[]{:S(2)}) async-start(f32[8,4,2,512]{3,2,1,0:T(2,128)} %broadcast_in_dim.21), calls=%async_computation | async-start | bytes 262144 | tf_op jit(solution)/shard_map/all_to_all | solution.py:15
  167.3 5.4 %all-to-all-done = f32[8,4,2,512]{3,2,1,0:T(2,128)S(1)} async-done(((f32[8,4,2,512]{3,2,1,0:T(2,128)}), f32[8,4,2,512]{3,2,1,0:T(2,128)S(1)}, u32[]{:S(2)}, u32[]{:S(2)}) %all-to-all-start) | async-done | bytes 131104 | tf_op jit(solution)/shard_map/all_to_all | solution.py:15
  172.7 0.5 fusion.1
  173.3 0.7 fusion.21
  174.0 5.4 %collective-permute-start.1 = (f32[34,8,1,128]{3,1,2,0:T(8,128)}, f32[34,8,1,128]{3,1,2,0:T(8,128)S(1)}, u32[]{:S(2)}, u32[]{:S(2)}) collective-permute-start(f32[34,8,1,128]{3,1,2,0:T(8,128)} %get-tuple-element.8), channel_id=1, source_target_pairs={{1,0},{2,1},{3,2},{4,3},{5,4},{6,5},{7,6},{8,7},{9,8},{10,9},{11,1... | collective-permute-start | bytes 417800 | tf_op jit(solution)/shard_map/ppermute | solution.py:38
  179.4 0.8 copy.12
  180.3 2.7 %gather_fusion.2 = f32[512,32,8]{1,2,0:T(8,128)} fusion(f32[32,8,512]{0,1,2:T(8,128)S(1)} %copy.12, s32[1024]{0:T(1024)S(1)} %pad_clamp_fusion), kind=kCustom, calls=%fused_computation.2 | custom fusion | bytes 1050624 | tf_op jit(solution)/shard_map/jit(_take)/gather | solution.py:60
  183.0 2.4 %copy.13 = f32[512,32,8]{0,2,1:T(8,128)S(1)} copy(f32[512,32,8]{1,2,0:T(8,128)} %gather_fusion.2) | data formatting | bytes 1048576 | tf_op jit(solution)/shard_map/jit(_take)/gather | solution.py:60
  185.4 0.1 pad_maximum_fusion
  185.5 0.2 fusion.3
  185.7 0.3 fusion.6
  186.0 1.0 fusion.11
  (17 shorter events, 0.1 us)
Async XLA Ops:
  6.5 107.1 %all-gather.2.cloned.1.call-start = ((), (), s32[]{:S(2)}) async-start(), calls=%async_computation.1 | async-start | bytes 8650752 | tf_op jit(solution)/shard_map/all_gather | solution.py:78
  8.2 9.6 %slice-start = ((bf16[8,512,1024]{2,1,0:T(8,128)(2,1)}), bf16[8,512,32]{2,1,0:T(8,128)(2,1)S(1)}, s32[]{:S(2)}) async-start(bf16[8,512,1024]{2,1,0:T(8,128)(2,1)} %param.5), calls=%async_computation.2 | async-start | bytes 2097152 | tf_op jit(solution)/shard_map/slice | solution.py:73
  8.3 10.1 %copy-start = (s32[512]{0:T(512)S(1)}, s32[512]{0:T(512)}, u32[]{:S(2)}) copy-start(s32[512]{0:T(512)} %param.8) | copy-start | bytes 6148
  150.1 17.2 %copy-start.1 = (f32[8]{0:T(128)S(1)}, f32[8]{0:T(128)}, u32[]{:S(2)}) copy-start(f32[8]{0:T(128)} %param.9) | copy-start | bytes 100
  161.6 11.2 %all-to-all-start = ((f32[8,4,2,512]{3,2,1,0:T(2,128)}), f32[8,4,2,512]{3,2,1,0:T(2,128)S(1)}, u32[]{:S(2)}, u32[]{:S(2)}) async-start(f32[8,4,2,512]{3,2,1,0:T(2,128)} %broadcast_in_dim.21), calls=%async_computation | async-start | bytes 262144 | tf_op jit(solution)/shard_map/all_to_all | solution.py:15
  174.0 11.4 %collective-permute-start = (f32[34,8,1,128]{3,1,2,0:T(8,128)}, f32[34,8,1,128]{3,1,2,0:T(8,128)S(1)}, u32[]{:S(2)}, u32[]{:S(2)}) collective-permute-start(f32[34,8,1,128]{3,1,2,0:T(8,128)} %get-tuple-element.9), channel_id=1, source_target_pairs={{0,1},{1,2},{2,3},{3,4},{4,5},{5,6},{6,7},{7,8},{8,9},{9,10},{10,1... | collective-permute-start | bytes 417800 | tf_op jit(solution)/shard_map/ppermute | solution.py:36
  174.0 11.4 %collective-permute-start.1 = (f32[34,8,1,128]{3,1,2,0:T(8,128)}, f32[34,8,1,128]{3,1,2,0:T(8,128)S(1)}, u32[]{:S(2)}, u32[]{:S(2)}) collective-permute-start(f32[34,8,1,128]{3,1,2,0:T(8,128)} %get-tuple-element.8), channel_id=1, source_target_pairs={{1,0},{2,1},{3,2},{4,3},{5,4},{6,5},{7,6},{8,7},{9,8},{10,9},{11,1... | collective-permute-start | bytes 417800 | tf_op jit(solution)/shard_map/ppermute | solution.py:38
Sparse Core Ops, SparseCore 0:
  10.2 103.4 all-gather.1
where the time goes:
time: 195 us; the launch traced here: 194 us
  waiting for transfers between devices  98.9 us (51%)
  local copies, waits for them, and re-layouts  38.2 us (20%)
  matrix products  16.6 us (9%)
  other arithmetic  15.5 us (8%)
  between operations  13.5 us (7%)
  starting transfers between devices  11.1 us (6%)
    all_gather x1, waiting for transfers between devices, local(): piece = lax.all_gather(tensor, 'brick', axis=1, tiled=True)  92.7 us
    reshape x1, local copies, waits for them, and re-layouts, local(): inner = inner.reshape(local_modes, rows_here, pair_count, cells)  20.4 us
    dot_general x1, matrix products, local(): lax.dot_general(piece.reshape(local_modes * rows_here, width), right_flat...  16 us
    reduce_sum x1, other arithmetic, local(): collide = jnp.sum(inner * factor[None], axis=1)  10.5 us
    all_to_all x1, starting transfers between devices, sent_to_all(): return lax.all_to_all(copies, axis, split_axis=0, concat_axis=0, tiled=True)  5.74 us
    gather x1, local copies, waits for them, and re-layouts, local(): right_flat = coeffs[pairs[:, 1]].reshape(pair_count * cells, width)  5.5 us
    all_to_all x1, waiting for transfers between devices, sent_to_all(): return lax.all_to_all(copies, axis, split_axis=0, concat_axis=0, tiled=True)  5.41 us
    ppermute x1, starting transfers between devices, with_halo(): lax.ppermute(head, axis, [((i + 1) % count, i) for i in range(count)])  5.36 us
  transfers between devices with their start and end apart: 4, of which 2 were waited for; matrix products, arithmetic and copies ran while one was open for 10% of the time, Pallas kernels for 0%

commit v1 on v0

--- a/solution.py
+++ b/solution.py
@@ -75,7 +75,9 @@
     indicator_matrix = (
         pairs[:, 0][:, None] == jnp.arange(species, dtype=jnp.int32)[None, :]
     ).astype(jnp.float32)
-    piece = lax.all_gather(tensor, "brick", axis=1, tiled=True)
+    piece = jnp.concatenate(
+        lax.all_to_all(jnp.stack([tensor] * lax.axis_size("brick")), "brick", 0, 0), axis=1
+    )
     rows_here = piece.shape[1]
     inner = lax.dot_general(
         piece.reshape(local_modes * rows_here, width),

time: 195 us -> 284 us (1.46)
  waiting for transfers between devices: 98.9 us -> 179 us
  local copies, waits for them, and re-layouts: 38.2 us -> 51.8 us
  between operations: 13.5 us -> 0.18 us
  starting transfers between devices: 11.1 us -> 22 us
    all_to_all x0 -> x1, waiting for transfers between devices: none -> 174 us  [local(): lax.all_to_all(jnp.stack([tensor] * lax.axis_size('brick')), 'brick', 0, 0)]
    all_gather x1 -> x0, waiting for transfers between devices: 92.7 us -> none  [local(): piece = lax.all_gather(tensor, 'brick', axis=1, tiled=True)]
    all_to_all x0 -> x1, starting transfers between devices: none -> 10.7 us  [local(): lax.all_to_all(jnp.stack([tensor] * lax.axis_size('brick')), 'brick', 0, 0)]
    all_to_all x0 -> x1, local copies, waits for them, and re-layouts: none -> 8.46 us  [local(): lax.all_to_all(jnp.stack([tensor] * lax.axis_size('brick')), 'brick', 0, 0)]
    another operation x0 -> x1, local copies, waits for them, and re-layouts: none -> 5.24 us  [local(): jnp.stack([tensor] * lax.axis_size('brick'))]
  transfers between devices with their start and end apart: 4 -> 4, of which waited for: 2 -> 2; matrix products, arithmetic and copies ran while one was open for 10% -> 7% of each run, Pallas kernels for 0% -> 0%
where the time goes in v1:
time: 284 us; the launch traced here: 283 us
  waiting for transfers between devices  179 us (63%)
  local copies, waits for them, and re-layouts  51.8 us (18%)
  starting transfers between devices  22 us (8%)
  matrix products  15 us (5%)
  other arithmetic  14.8 us (5%)
    all_to_all x1, waiting for transfers between devices, local(): lax.all_to_all(jnp.stack([tensor] * lax.axis_size('brick')), 'brick', 0, 0)  174 us
    reshape x1, local copies, waits for them, and re-layouts, local(): inner = inner.reshape(local_modes, rows_here, pair_count, cells)  20.4 us
    dot_general x1, matrix products, local(): lax.dot_general(piece.reshape(local_modes * rows_here, width), right_flat...  14.5 us
    all_to_all x1, starting transfers between devices, local(): lax.all_to_all(jnp.stack([tensor] * lax.axis_size('brick')), 'brick', 0, 0)  10.7 us
    reduce_sum x1, other arithmetic, local(): collide = jnp.sum(inner * factor[None], axis=1)  10.5 us
    all_to_all x1, local copies, waits for them, and re-layouts, local(): lax.all_to_all(jnp.stack([tensor] * lax.axis_size('brick')), 'brick', 0, 0)  8.46 us
    all_to_all x1, starting transfers between devices, sent_to_all(): return lax.all_to_all(copies, axis, split_axis=0, concat_axis=0, tiled=True)  5.93 us
  transfers between devices with their start and end apart: 4, of which 2 were waited for; matrix products, arithmetic and copies ran while one was open for 7% of the time, Pallas kernels for 0%

profile of v1, /device:TPU:2, one launch (start us, length us, event | category | flops | bytes accessed | tf_op | source)
XLA Modules:
  0.0 283.0 jit_solution(6457531115935615496)
XLA Ops:
  0.0 5.2 %stack.2 = bf16[32,4,32,1024]{3,2,1,0:T(8,128)(2,1)} broadcast(bf16[4,32,1024]{2,1,0:T(8,128)(2,1)} %param.6), dimensions={1,2,3} | broadcast | bytes 8650752 | tf_op jit(solution)/shard_map/stack | solution.py:79
  5.2 10.7 %all-to-all-start = ((bf16[32,4,32,1024]{3,2,1,0:T(8,128)(2,1)}), bf16[32,4,32,1024]{3,2,1,0:T(8,128)(2,1)}, u32[]{:S(2)}, u32[]{:S(2)}) async-start(bf16[32,4,32,1024]{3,2,1,0:T(8,128)(2,1)} %stack.2), calls=%async_computation | async-start | bytes 16777216 | tf_op jit(solution)/shard_map/all_to_all | solution.py:79
  16.2 5.5 %gather_fusion = bf16[2,512,1024]{2,1,0:T(8,128)(2,1)} fusion(bf16[8,512,1024]{2,1,0:T(8,128)(2,1)} %param.5, s32[1024]{0:T(1024)S(1)} %get-tuple-element.11), kind=kCustom, calls=%fused_computation | custom fusion | bytes 4194312 | tf_op jit(solution)/shard_map/gather | solution.py:72
  21.6 4.1 %gather_fusion.1 = bf16[2,512,1024]{2,1,0:T(8,128)(2,1)S(1)} fusion(bf16[8,512,1024]{2,1,0:T(8,128)(2,1)} %param.5, s32[1024]{0:T(1024)S(1)} %get-tuple-element.10), kind=kCustom, calls=%fused_computation.1 | custom fusion | bytes 4194312 | tf_op jit(solution)/shard_map/gather | solution.py:71
  25.7 0.5 copy.15
  26.3 2.5 convert_bitcast_fusion
  28.8 173.8 %all-to-all-done = bf16[32,4,32,1024]{3,2,1,0:T(8,128)(2,1)} async-done(((bf16[32,4,32,1024]{3,2,1,0:T(8,128)(2,1)}), bf16[32,4,32,1024]{3,2,1,0:T(8,128)(2,1)}, u32[]{:S(2)}, u32[]{:S(2)}) %all-to-all-start) | async-done | bytes 8388640 | tf_op jit(solution)/shard_map/all_to_all | solution.py:79
  202.6 8.5 %copy.11 = bf16[32,4,32,1024]{3,2,0,1:T(8,128)(2,1)} copy(bf16[32,4,32,1024]{3,2,1,0:T(8,128)(2,1)} %all-to-all-done) | data formatting | bytes 16777216 | tf_op jit(solution)/shard_map/all_to_all | solution.py:79
  211.1 14.5 %convolution_bitcast_fusion = f32[4096,1024]{0,1:T(8,128)} fusion(bf16[1024,1024]{1,0:T(8,128)(2,1)S(1)} %bitcast.38, bf16[4096,1024]{1,0:T(8,128)(2,1)} %bitcast.37), kind=kOutput, calls=%fused_computation.4 | convolution fusion | flops 8589934592 | bytes 27262976 | tf_op jit(solution)/shard_map/dot_general | solution.py:82
  225.6 20.4 %reshape.46 = f32[4,1024,2,512]{1,0,3,2:T(4,128)} reshape(f32[4096,1024]{0,1:T(8,128)} %convolution_bitcast_fusion) | data formatting | bytes 33554432 | tf_op jit(solution)/shard_map/reshape | solution.py:88
  246.0 10.5 %multiply_reduce_fusion = f32[4,2,512]{0,2,1:T(8,128)S(1)} fusion(f32[4,1024,2,512]{1,0,3,2:T(4,128)} %reshape.46, f32[1024,2,512]{0,2,1:T(8,128)} %convert_bitcast_fusion), kind=kLoop, calls=%fused_computation.3 | loop fusion | flops 8384512 | bytes 20987904 | tf_op jit(solution)/shard_map/reduce_sum | solution.py:90
  256.6 0.2 copy.12
  256.8 0.7 broadcast_in_dim.21
  257.5 5.9 %all-to-all-start.1 = ((f32[8,4,2,512]{3,2,1,0:T(2,128)}), f32[8,4,2,512]{3,2,1,0:T(2,128)S(1)}, u32[]{:S(2)}, u32[]{:S(2)}) async-start(f32[8,4,2,512]{3,2,1,0:T(2,128)} %broadcast_in_dim.21), calls=%async_computation.1 | async-start | bytes 262144 | tf_op jit(solution)/shard_map/all_to_all | solution.py:15
  263.4 5.4 %all-to-all-done.1 = f32[8,4,2,512]{3,2,1,0:T(2,128)S(1)} async-done(((f32[8,4,2,512]{3,2,1,0:T(2,128)}), f32[8,4,2,512]{3,2,1,0:T(2,128)S(1)}, u32[]{:S(2)}, u32[]{:S(2)}) %all-to-all-start.1) | async-done | bytes 131104 | tf_op jit(solution)/shard_map/all_to_all | solution.py:15
  268.8 0.5 fusion.1
  269.3 0.7 fusion.21
  270.1 5.4 %collective-permute-start.1 = (f32[34,8,1,128]{3,1,2,0:T(8,128)}, f32[34,8,1,128]{3,1,2,0:T(8,128)S(1)}, u32[]{:S(2)}, u32[]{:S(2)}) collective-permute-start(f32[34,8,1,128]{3,1,2,0:T(8,128)} %get-tuple-element.8), channel_id=1, source_target_pairs={{1,0},{2,1},{3,2},{4,3},{5,4},{6,5},{7,6},{8,7},{9,8},{10,9},{11,1... | collective-permute-start | bytes 417800 | tf_op jit(solution)/shard_map/ppermute | solution.py:38
  275.5 0.8 copy.13
  276.3 2.7 gather_fusion.2
  279.1 2.4 copy.14
  281.5 0.2 fusion.3
  281.7 0.3 fusion.6
  282.0 1.0 fusion.11
  (22 shorter events, 0.3 us)
Async XLA Ops:
  5.2 10.7 %copy-start.2 = (s32[2,2]{1,0:T(2,128)S(1)}, s32[2,2]{1,0:T(2,128)}, u32[]{:S(2)}) copy-start(s32[2,2]{1,0:T(2,128)} %param.7) | copy-start | bytes 52
  5.2 197.4 %all-to-all-start = ((bf16[32,4,32,1024]{3,2,1,0:T(8,128)(2,1)}), bf16[32,4,32,1024]{3,2,1,0:T(8,128)(2,1)}, u32[]{:S(2)}, u32[]{:S(2)}) async-start(bf16[32,4,32,1024]{3,2,1,0:T(8,128)(2,1)} %stack.2), calls=%async_computation | async-start | bytes 16777216 | tf_op jit(solution)/shard_map/all_to_all | solution.py:79
  16.1 9.6 %slice-start = ((bf16[8,512,1024]{2,1,0:T(8,128)(2,1)}), bf16[8,512,32]{2,1,0:T(8,128)(2,1)S(1)}, s32[]{:S(2)}) async-start(bf16[8,512,1024]{2,1,0:T(8,128)(2,1)} %param.5), calls=%async_computation.2 | async-start | bytes 2097152 | tf_op jit(solution)/shard_map/slice | solution.py:73
  16.1 10.1 %copy-start.1 = (s32[512]{0:T(512)S(1)}, s32[512]{0:T(512)}, u32[]{:S(2)}) copy-start(s32[512]{0:T(512)} %param.8) | copy-start | bytes 6148
  28.8 182.3 %copy-start = (bf16[2,512,1024]{2,1,0:T(8,128)(2,1)S(1)}, bf16[2,512,1024]{2,1,0:T(8,128)(2,1)}, u32[]{:S(2)}) copy-start(bf16[2,512,1024]{2,1,0:T(8,128)(2,1)} %gather_fusion) | copy-start | bytes 6291460
  246.0 17.4 %copy-start.3 = (f32[8]{0:T(128)S(1)}, f32[8]{0:T(128)}, u32[]{:S(2)}) copy-start(f32[8]{0:T(128)} %param.9) | copy-start | bytes 100
  257.5 11.3 %all-to-all-start.1 = ((f32[8,4,2,512]{3,2,1,0:T(2,128)}), f32[8,4,2,512]{3,2,1,0:T(2,128)S(1)}, u32[]{:S(2)}, u32[]{:S(2)}) async-start(f32[8,4,2,512]{3,2,1,0:T(2,128)} %broadcast_in_dim.21), calls=%async_computation.1 | async-start | bytes 262144 | tf_op jit(solution)/shard_map/all_to_all | solution.py:15
  270.1 11.4 %collective-permute-start = (f32[34,8,1,128]{3,1,2,0:T(8,128)}, f32[34,8,1,128]{3,1,2,0:T(8,128)S(1)}, u32[]{:S(2)}, u32[]{:S(2)}) collective-permute-start(f32[34,8,1,128]{3,1,2,0:T(8,128)} %get-tuple-element.9), channel_id=1, source_target_pairs={{0,1},{1,2},{2,3},{3,4},{4,5},{5,6},{6,7},{7,8},{8,9},{9,10},{10,1... | collective-permute-start | bytes 417800 | tf_op jit(solution)/shard_map/ppermute | solution.py:36
  270.1 11.4 %collective-permute-start.1 = (f32[34,8,1,128]{3,1,2,0:T(8,128)}, f32[34,8,1,128]{3,1,2,0:T(8,128)S(1)}, u32[]{:S(2)}, u32[]{:S(2)}) collective-permute-start(f32[34,8,1,128]{3,1,2,0:T(8,128)} %get-tuple-element.8), channel_id=1, source_target_pairs={{1,0},{2,1},{3,2},{4,3},{5,4},{6,5},{7,6},{8,7},{9,8},{10,9},{11,1... | collective-permute-start | bytes 417800 | tf_op jit(solution)/shard_map/ppermute | solution.py:38
